TPU v7x, 32 devices: a whole 2x2x4 slice. The times are simulated.
32 devices in a mesh: frame: 4 (over y, x), row: 8 (over z, core).
Axes of the slice: x: 2, y: 2, z: 4, core: 2. Of those that a mesh axis runs over, the one named last changes fastest.
Arguments:
- frames_in: bfloat16 [8, 32, 32, 256], P('frame', 'row'), may hold values from -6 to 6
- conv_first: bfloat16 [3, 3, 256, 256], replicated, may hold values from -0.125 to 0.125
- conv_second: bfloat16 [3, 3, 256, 256], replicated, may hold values from -0.125 to 0.125
- time_kernel: bfloat16 [3, 256, 256], replicated, may hold values from -0.21875 to 0.21875
- norm_gain: float32 [256], replicated, may hold values from 0.1 to 1.9
- w_query: bfloat16 [256, 256], replicated, may hold values from -0.375 to 0.375
- w_key: bfloat16 [256, 256], replicated, may hold values from -0.375 to 0.375
- w_value: bfloat16 [256, 256], replicated, may hold values from -0.375 to 0.375
- w_out: bfloat16 [256, 256], replicated, may hold values from -0.375 to 0.375
- frame_bias: float32 [8, 8], replicated, may hold values from -6 to 400
- conv_third: bfloat16 [3, 3, 256, 256], replicated, may hold values from -0.125 to 0.125
Outputs:
- encoded: bfloat16 [8, 32, 32, 256], P(None, 'row', 'frame')
All inputs are finite; a program needn't handle non-finite values.
Results may differ from a plain program's by a relative error of at most 0.018.
Values may be sent and summed in bfloat16 or wider, within the bound.
A program may use at most 64 MiB of HBM per device.

v0:
```python
import math
import jax
import jax.numpy as jnp
from jax import lax
from jax.sharding import PartitionSpec as P


def extended(cells, sides, width):
    for axis, dim in sides:
        count = lax.axis_size(axis)
        ends = count - 1
        head = lax.slice_in_dim(cells, 0, width, axis=dim)
        tail = lax.slice_in_dim(cells, cells.shape[dim] - width, cells.shape[dim], axis=dim)
        cells = jnp.concatenate(
            [
                lax.ppermute(tail, axis, [(i, (i + 1) % count) for i in range(ends)]),
                cells,
                lax.ppermute(head, axis, [((i + 1) % count, i) for i in range(ends)]),
            ],
            axis=dim,
        )
    return cells


def spatial(padded, weight, row_count, col_count):
    channels = weight.shape[2]
    summed = jnp.zeros((padded.shape[0] * row_count * col_count, weight.shape[3]), jnp.float32)
    for row_tap in range(3):
        for col_tap in range(3):
            window = padded[:, row_tap : row_tap + row_count, col_tap : col_tap + col_count, :]
            summed = summed + jnp.dot(
                window.reshape(-1, channels),
                weight[row_tap, col_tap],
                preferred_element_type=jnp.float32,
            )
    return summed.reshape(padded.shape[0], row_count, col_count, weight.shape[3])


def pad_columns(field):
    return jnp.pad(field, ((0, 0), (0, 0), (1, 1), (0, 0)))


def temporal(moved, time_kernel, norm_gain, w_query, w_key, w_value, w_out, frame_bias):
    frame_count = moved.shape[0]
    channels = moved.shape[-1]
    pixels = moved.reshape(frame_count, -1, channels)
    padded = jnp.pad(pixels, ((1, 1), (0, 0), (0, 0)))
    summed = pixels.astype(jnp.float32)
    for tap in range(3):
        shifted = padded[tap : tap + frame_count].reshape(-1, channels)
        summed = summed + jnp.dot(
            shifted, time_kernel[tap], preferred_element_type=jnp.float32
        ).reshape(pixels.shape)
    timed = summed.astype(jnp.bfloat16)
    widened = timed.astype(jnp.float32)
    scale_inv = lax.rsqrt(jnp.mean(widened * widened, axis=-1, keepdims=True) + 1e-06)
    normed = (widened * scale_inv * norm_gain).astype(jnp.bfloat16).reshape(-1, channels)
    queries = (
        jnp.dot(normed, w_query, preferred_element_type=jnp.float32)
        .astype(jnp.bfloat16)
        .reshape(pixels.shape)
    )
    key_rows = (
        jnp.dot(normed, w_key, preferred_element_type=jnp.float32)
        .astype(jnp.bfloat16)
        .reshape(pixels.shape)
    )
    value_rows = (
        jnp.dot(normed, w_value, preferred_element_type=jnp.float32)
        .astype(jnp.bfloat16)
        .reshape(pixels.shape)
    )
    scores = jnp.einsum(
        "fpc,gpc->pfg", queries, key_rows, preferred_element_type=jnp.float32
    ) / math.sqrt(channels)
    scores = scores + frame_bias
    peak = jnp.max(scores, axis=-1, keepdims=True)
    raised = jnp.exp(scores - peak)
    probs = (raised / jnp.sum(raised, axis=-1, keepdims=True)).astype(jnp.bfloat16)
    context = jnp.einsum(
        "pfg,gpc->fpc", probs, value_rows, preferred_element_type=jnp.float32
    ).astype(jnp.bfloat16)
    projected = jnp.dot(
        context.reshape(-1, channels), w_out, preferred_element_type=jnp.float32
    ).reshape(pixels.shape)
    return (widened + projected).astype(jnp.bfloat16).reshape(moved.shape)


def on_device(
    frames_in,
    conv_first,
    conv_second,
    time_kernel,
    norm_gain,
    w_query,
    w_key,
    w_value,
    w_out,
    frame_bias,
    conv_third,
):
    row_count = frames_in.shape[1]
    col_whole = frames_in.shape[2]
    haloed = extended(frames_in, (("row", 1),), 1)
    first = jax.nn.silu(spatial(pad_columns(haloed), conv_first, row_count, col_whole)).astype(
        jnp.bfloat16
    )
    haloed_two = extended(first, (("row", 1),), 1)
    second = jax.nn.silu(
        spatial(pad_columns(haloed_two), conv_second, row_count, col_whole)
    ).astype(jnp.bfloat16)
    moved = lax.all_to_all(second, "frame", split_axis=2, concat_axis=0, tiled=True)
    attended = temporal(moved, time_kernel, norm_gain, w_query, w_key, w_value, w_out, frame_bias)
    col_count = attended.shape[2]
    framed_last = extended(attended, (("frame", 2), ("row", 1)), 1)
    return spatial(framed_last, conv_third, row_count, col_count).astype(jnp.bfloat16)


def solution(mesh):
    placed = (P("frame", "row", None, None), P(), P(), P(), P(), P(), P(), P(), P(), P(), P())
    return jax.shard_map(
        on_device,
        mesh=mesh,
        in_specs=placed,
        out_specs=P(None, "row", "frame", None),
        check_vma=False,
    )
```

profile of v0, /device:TPU:21, one launch (start us, length us, event | category | flops | bytes accessed | tf_op | source)
XLA Modules:
  0.0 54.3 jit_solution(5470945481003135327)
XLA Ops:
  0.0 0.9 %fusion.102 = (bf16[2,1,32,256]{3,2,1,0:T(8,128)(2,1)S(1)}, bf16[2,1,32,256]{3,2,1,0:T(8,128)(2,1)S(1)}) fusion(bf16[2,4,32,256]{3,2,1,0:T(8,128)(2,1)} %param.11), kind=kLoop, calls=%fused_computation.152 | loop fusion | bytes 131072 | tf_op jit(solution)/shard_map/slice | solution.py:13
  0.9 2.6 %collective-permute-start.1 = (bf16[2,1,32,256]{3,2,1,0:T(8,128)(2,1)S(1)}, bf16[2,1,32,256]{3,2,1,0:T(8,128)(2,1)S(1)}, u32[]{:S(2)}, u32[]{:S(2)}) collective-permute-start(bf16[2,1,32,256]{3,2,1,0:T(8,128)(2,1)S(1)} %get-tuple-element.38), channel_id=1, source_target_pairs={{1,0},{2,1},{3,2},{4,3},{5,4},{6,5},{7,6},{9,8},{10,9},{11,10},{12... | collective-permute-start | bytes 98312 | tf_op jit(solution)/shard_map/ppermute | solution.py:18
  3.5 3.1 %collective-permute-start = (bf16[2,1,32,256]{3,2,1,0:T(8,128)(2,1)S(1)}, bf16[2,1,32,256]{3,2,1,0:T(8,128)(2,1)S(1)}, u32[]{:S(2)}, u32[]{:S(2)}) collective-permute-start(bf16[2,1,32,256]{3,2,1,0:T(8,128)(2,1)S(1)} %get-tuple-element.37), channel_id=1, source_target_pairs={{0,1},{1,2},{2,3},{3,4},{4,5},{5,6},{6,7},{8,9},{9,10},{10,11},{11... | collective-permute-start | bytes 98312 | tf_op jit(solution)/shard_map/ppermute | solution.py:16
  6.6 1.0 %collective-permute-done = bf16[2,1,32,256]{3,2,1,0:T(8,128)(2,1)S(1)} collective-permute-done((bf16[2,1,32,256]{3,2,1,0:T(8,128)(2,1)S(1)}, bf16[2,1,32,256]{3,2,1,0:T(8,128)(2,1)S(1)}, u32[]{:S(2)}, u32[]{:S(2)}) %collective-permute-start) | collective-permute-done | bytes 32800 | tf_op jit(solution)/shard_map/ppermute | solution.py:16
  7.6 1.0 %fusion.19 = bf16[2,6,34,256]{3,2,1,0:T(8,128)(2,1)S(1)} fusion(bf16[2,1,32,256]{3,2,1,0:T(8,128)(2,1)S(1)} %collective-permute-done.1, bf16[2,4,32,256]{3,2,1,0:T(8,128)(2,1)} %param.11, bf16[2,1,32,256]{3,2,1,0:T(8,128)(2,1)S(1)} %collective-permute-done), kind=kLoop, calls=%fused_computation.58 | loop fusion | flops 1253376 | bytes 405504 | tf_op jit(solution)/shard_map/concatenate | solution.py:14
  8.6 0.1 fusion.99
  8.7 0.2 fusion.48
  8.9 0.2 fusion.57
  9.1 0.4 copy-done.1
  9.5 0.2 convolution_add_fusion.22
  9.7 0.2 convolution_add_fusion.21
  9.9 0.2 convolution_add_fusion.20
  10.1 0.2 convolution_add_fusion.19
  10.3 0.2 convolution_add_fusion.18
  10.5 0.2 convolution_add_fusion.17
  10.7 0.2 fusion.5
  10.9 0.1 multiply_convert_fusion.3
  11.0 3.2 %collective-permute-start.3 = (bf16[2,1,32,256]{3,2,1,0:T(8,128)(2,1)S(1)}, bf16[2,1,32,256]{3,2,1,0:T(8,128)(2,1)S(1)}, u32[]{:S(2)}, u32[]{:S(2)}) collective-permute-start(bf16[2,1,32,256]{3,2,1,0:T(8,128)(2,1)S(1)} %get-tuple-element.34), channel_id=1, source_target_pairs={{1,0},{2,1},{3,2},{4,3},{5,4},{6,5},{7,6},{9,8},{10,9},{11,10},{12... | collective-permute-start | bytes 98312 | tf_op jit(solution)/shard_map/ppermute | solution.py:18
  14.2 3.1 %collective-permute-start.2 = (bf16[2,1,32,256]{3,2,1,0:T(8,128)(2,1)S(1)}, bf16[2,1,32,256]{3,2,1,0:T(8,128)(2,1)S(1)}, u32[]{:S(2)}, u32[]{:S(2)}) collective-permute-start(bf16[2,1,32,256]{3,2,1,0:T(8,128)(2,1)S(1)} %get-tuple-element.33), channel_id=1, source_target_pairs={{0,1},{1,2},{2,3},{3,4},{4,5},{5,6},{6,7},{8,9},{9,10},{10,11},{11... | collective-permute-start | bytes 98312 | tf_op jit(solution)/shard_map/ppermute | solution.py:16
  17.3 1.0 %collective-permute-done.2 = bf16[2,1,32,256]{3,2,1,0:T(8,128)(2,1)S(1)} collective-permute-done((bf16[2,1,32,256]{3,2,1,0:T(8,128)(2,1)S(1)}, bf16[2,1,32,256]{3,2,1,0:T(8,128)(2,1)S(1)}, u32[]{:S(2)}, u32[]{:S(2)}) %collective-permute-start.2) | collective-permute-done | bytes 32800 | tf_op jit(solution)/shard_map/ppermute | solution.py:16
  18.3 0.1 select_maximum_fusion
  18.4 0.1 fusion.98
  18.5 0.2 fusion.37
  18.7 0.2 fusion.46
  18.9 0.2 convolution_add_fusion.15
  19.1 0.2 convolution_add_fusion.14
  19.3 0.2 convolution_add_fusion.13
  19.5 0.2 convolution_add_fusion.12
  19.7 0.2 convolution_add_fusion.11
  19.9 0.2 convolution_add_fusion.10
  20.1 0.2 fusion.4
  20.3 0.1 multiply_convert_fusion.1
  20.4 0.8 %copy.24 = bf16[2,4,32,256]{3,1,0,2:T(4,128)(2,1)} copy(bf16[2,4,32,256]{3,2,1,0:T(8,128)(2,1)S(1)} %multiply_convert_fusion.1) | data formatting | bytes 262144 | tf_op jit(solution)/shard_map/convert_element_type | solution.py:111
  21.1 3.7 %all-to-all-start = ((bf16[2,4,32,256]{3,1,0,2:T(4,128)(2,1)}), bf16[2,4,32,256]{3,1,0,2:T(4,128)(2,1)S(1)}, u32[]{:S(2)}, u32[]{:S(2)}) async-start(bf16[2,4,32,256]{3,1,0,2:T(4,128)(2,1)} %copy.24), calls=%async_computation | async-start | bytes 262144 | tf_op jit(solution)/shard_map/all_to_all | solution.py:112
  24.9 3.3 %all-to-all-done = bf16[2,4,32,256]{3,1,0,2:T(4,128)(2,1)S(1)} async-done(((bf16[2,4,32,256]{3,1,0,2:T(4,128)(2,1)}), bf16[2,4,32,256]{3,1,0,2:T(4,128)(2,1)S(1)}, u32[]{:S(2)}, u32[]{:S(2)}) %all-to-all-start) | async-done | bytes 131104 | tf_op jit(solution)/shard_map/all_to_all | solution.py:112
  28.2 0.2 fusion.34
  28.4 0.2 fusion.1
  28.6 0.3 multiply_reduce_fusion
  28.9 0.1 multiply_convert_fusion
  29.0 0.2 convolution_convert_fusion.3
  29.3 0.2 convolution_convert_fusion.1
  29.5 0.2 convolution_convert_fusion.2
  29.7 0.3 fusion.13
  30.0 0.1 fusion.103
  30.0 0.3 fusion.11
  30.3 0.2 fusion.6
  30.6 2.8 %collective-permute-start.5 = (bf16[8,4,1,256]{3,2,1,0:T(2,128)(2,1)S(1)}, bf16[8,4,1,256]{3,2,1,0:T(2,128)(2,1)S(1)}, u32[]{:S(2)}, u32[]{:S(2)}) collective-permute-start(bf16[8,4,1,256]{3,2,1,0:T(2,128)(2,1)S(1)} %get-tuple-element.30), channel_id=1, source_target_pairs={{8,0},{16,8},{24,16},{9,1},{17,9},{25,17},{10,2},{18,10},{26,18},{... | collective-permute-start | bytes 49160 | tf_op jit(solution)/shard_map/ppermute | solution.py:18
  33.4 2.5 %collective-permute-start.4 = (bf16[8,4,1,256]{3,2,1,0:T(2,128)(2,1)S(1)}, bf16[8,4,1,256]{3,2,1,0:T(2,128)(2,1)S(1)}, u32[]{:S(2)}, u32[]{:S(2)}) collective-permute-start(bf16[8,4,1,256]{3,2,1,0:T(2,128)(2,1)S(1)} %get-tuple-element.29), channel_id=1, source_target_pairs={{0,8},{8,16},{16,24},{1,9},{9,17},{17,25},{2,10},{10,18},{18,26},{... | collective-permute-start | bytes 49160 | tf_op jit(solution)/shard_map/ppermute | solution.py:16
  35.9 0.2 fusion.25
  36.1 2.9 %collective-permute-done.4 = bf16[8,4,1,256]{3,2,1,0:T(2,128)(2,1)S(1)} collective-permute-done((bf16[8,4,1,256]{3,2,1,0:T(2,128)(2,1)S(1)}, bf16[8,4,1,256]{3,2,1,0:T(2,128)(2,1)S(1)}, u32[]{:S(2)}, u32[]{:S(2)}) %collective-permute-start.4) | collective-permute-done | bytes 16416 | tf_op jit(solution)/shard_map/ppermute | solution.py:16
  39.0 7.1 %collective-permute-start.6 = (bf16[8,1,10,256]{3,2,1,0:T(8,128)(2,1)S(1)}, bf16[8,1,10,256]{3,2,1,0:T(8,128)(2,1)S(1)}, u32[]{:S(2)}, u32[]{:S(2)}) collective-permute-start(bf16[8,1,10,256]{3,2,1,0:T(8,128)(2,1)S(1)} %get-tuple-element.25), channel_id=1, source_target_pairs={{0,1},{1,2},{2,3},{3,4},{4,5},{5,6},{6,7},{8,9},{9,10},{10,11},{11... | collective-permute-start | bytes 122888 | tf_op jit(solution)/shard_map/ppermute | solution.py:16
  46.1 1.9 %collective-permute-start.7 = (bf16[8,1,10,256]{3,2,1,0:T(8,128)(2,1)S(1)}, bf16[8,1,10,256]{3,2,1,0:T(8,128)(2,1)S(1)}, u32[]{:S(2)}, u32[]{:S(2)}) collective-permute-start(bf16[8,1,10,256]{3,2,1,0:T(8,128)(2,1)S(1)} %get-tuple-element.26), channel_id=1, source_target_pairs={{1,0},{2,1},{3,2},{4,3},{5,4},{6,5},{7,6},{9,8},{10,9},{11,10},{12... | collective-permute-start | bytes 122888 | tf_op jit(solution)/shard_map/ppermute | solution.py:18
  48.0 0.1 pad_maximum_fusion.1
  48.2 3.5 %collective-permute-done.7 = bf16[8,1,10,256]{3,2,1,0:T(8,128)(2,1)S(1)} collective-permute-done((bf16[8,1,10,256]{3,2,1,0:T(8,128)(2,1)S(1)}, bf16[8,1,10,256]{3,2,1,0:T(8,128)(2,1)S(1)}, u32[]{:S(2)}, u32[]{:S(2)}) %collective-permute-start.7) | collective-permute-done | bytes 40992 | tf_op jit(solution)/shard_map/ppermute | solution.py:18
  51.7 0.3 maximum_maximum_fusion
  52.0 0.2 fusion.96
  52.1 0.2 fusion.22
  52.3 0.2 fusion.29
  52.5 0.2 convolution_add_fusion.7
  52.7 0.2 convolution_add_fusion.6
  52.9 0.2 fusion.3
  53.1 0.2 fusion.2
  53.3 0.2 convolution_add_fusion.3
  53.5 0.8 %fusion.7 = bf16[256,256]{1,0:T(8,128)(2,1)} fusion(f32[256,256]{1,0:T(8,128)S(1)} %convolution_add_fusion.3, bf16[256,256]{1,0:T(8,128)(2,1)S(1)} %bitcast.189, bf16[3,3,256,256]{3,2,1,0:T(8,128)(2,1)S(1)} %copy-done.3), kind=kOutput, calls=%fused_computation.30 | convolution fusion | flops 33685504 | bytes 655360 | tf_op jit(solution)/shard_map/dot_general | solution.py:31
  (33 shorter events, 0.4 us)
Async XLA Ops:
  0.0 29.0 %copy-start = (bf16[256,256]{1,0:T(8,128)(2,1)S(1)}, bf16[256,256]{1,0:T(8,128)(2,1)}, u32[]{:S(2)}) copy-start(bf16[256,256]{1,0:T(8,128)(2,1)} %param.18) | copy-start | bytes 393220
  0.0 8.7 %copy-start.2 = (bf16[3,3,256,256]{3,2,1,0:T(8,128)(2,1)S(1)}, bf16[3,3,256,256]{3,2,1,0:T(8,128)(2,1)}, u32[]{:S(2)}) copy-start(bf16[3,3,256,256]{3,2,1,0:T(8,128)(2,1)} %param.12) | copy-start | bytes 3538948
  0.9 5.7 %collective-permute-start.1 = (bf16[2,1,32,256]{3,2,1,0:T(8,128)(2,1)S(1)}, bf16[2,1,32,256]{3,2,1,0:T(8,128)(2,1)S(1)}, u32[]{:S(2)}, u32[]{:S(2)}) collective-permute-start(bf16[2,1,32,256]{3,2,1,0:T(8,128)(2,1)S(1)} %get-tuple-element.38), channel_id=1, source_target_pairs={{1,0},{2,1},{3,2},{4,3},{5,4},{6,5},{7,6},{9,8},{10,9},{11,10},{12... | collective-permute-start | bytes 98312 | tf_op jit(solution)/shard_map/ppermute | solution.py:18
  3.5 4.1 %collective-permute-start = (bf16[2,1,32,256]{3,2,1,0:T(8,128)(2,1)S(1)}, bf16[2,1,32,256]{3,2,1,0:T(8,128)(2,1)S(1)}, u32[]{:S(2)}, u32[]{:S(2)}) collective-permute-start(bf16[2,1,32,256]{3,2,1,0:T(8,128)(2,1)S(1)} %get-tuple-element.37), channel_id=1, source_target_pairs={{0,1},{1,2},{2,3},{3,4},{4,5},{5,6},{6,7},{8,9},{9,10},{10,11},{11... | collective-permute-start | bytes 98312 | tf_op jit(solution)/shard_map/ppermute | solution.py:16
  8.6 0.9 %copy-start.1 = (bf16[2,4,32,256]{3,2,1,0:T(8,128)(2,1)S(1)}, bf16[2,4,32,256]{3,2,1,0:T(8,128)(2,1)}, u32[]{:S(2)}) copy-start(bf16[2,4,32,256]{3,2,1,0:T(8,128)(2,1)} %param.11) | copy-start | bytes 393220
  10.9 7.6 %copy-start.4 = (bf16[3,3,256,256]{3,2,1,0:T(8,128)(2,1)S(1)}, bf16[3,3,256,256]{3,2,1,0:T(8,128)(2,1)}, u32[]{:S(2)}) copy-start(bf16[3,3,256,256]{3,2,1,0:T(8,128)(2,1)} %param.13) | copy-start | bytes 3538948
  11.0 6.3 %collective-permute-start.3 = (bf16[2,1,32,256]{3,2,1,0:T(8,128)(2,1)S(1)}, bf16[2,1,32,256]{3,2,1,0:T(8,128)(2,1)S(1)}, u32[]{:S(2)}, u32[]{:S(2)}) collective-permute-start(bf16[2,1,32,256]{3,2,1,0:T(8,128)(2,1)S(1)} %get-tuple-element.34), channel_id=1, source_target_pairs={{1,0},{2,1},{3,2},{4,3},{5,4},{6,5},{7,6},{9,8},{10,9},{11,10},{12... | collective-permute-start | bytes 98312 | tf_op jit(solution)/shard_map/ppermute | solution.py:18
  14.2 4.1 %collective-permute-start.2 = (bf16[2,1,32,256]{3,2,1,0:T(8,128)(2,1)S(1)}, bf16[2,1,32,256]{3,2,1,0:T(8,128)(2,1)S(1)}, u32[]{:S(2)}, u32[]{:S(2)}) collective-permute-start(bf16[2,1,32,256]{3,2,1,0:T(8,128)(2,1)S(1)} %get-tuple-element.33), channel_id=1, source_target_pairs={{0,1},{1,2},{2,3},{3,4},{4,5},{5,6},{6,7},{8,9},{9,10},{10,11},{11... | collective-permute-start | bytes 98312 | tf_op jit(solution)/shard_map/ppermute | solution.py:16
  20.1 4.7 %copy-start.9 = (f32[8,8]{1,0:T(8,128)S(1)}, f32[8,8]{1,0:T(8,128)}, u32[]{:S(2)}) copy-start(f32[8,8]{1,0:T(8,128)} %param.20) | copy-start | bytes 772
  20.1 8.1 %copy-start.5 = (bf16[3,256,256]{2,1,0:T(8,128)(2,1)S(1)}, bf16[3,256,256]{2,1,0:T(8,128)(2,1)}, u32[]{:S(2)}) copy-start(bf16[3,256,256]{2,1,0:T(8,128)(2,1)} %param.14) | copy-start | bytes 1179652
  21.1 7.0 %all-to-all-start = ((bf16[2,4,32,256]{3,1,0,2:T(4,128)(2,1)}), bf16[2,4,32,256]{3,1,0,2:T(4,128)(2,1)S(1)}, u32[]{:S(2)}, u32[]{:S(2)}) async-start(bf16[2,4,32,256]{3,1,0,2:T(4,128)(2,1)} %copy.24), calls=%async_computation | async-start | bytes 262144 | tf_op jit(solution)/shard_map/all_to_all | solution.py:112
  28.1 0.7 %copy-start.10 = (f32[256]{0:T(256)S(1)}, f32[256]{0:T(256)}, u32[]{:S(2)}) copy-start(f32[256]{0:T(256)} %param.15) | copy-start | bytes 3076
  28.4 0.9 %copy-start.6 = (bf16[256,256]{1,0:T(8,128)(2,1)S(1)}, bf16[256,256]{1,0:T(8,128)(2,1)}, u32[]{:S(2)}) copy-start(bf16[256,256]{1,0:T(8,128)(2,1)} %param.17) | copy-start | bytes 393220
  28.6 0.9 %copy-start.7 = (bf16[256,256]{1,0:T(8,128)(2,1)S(1)}, bf16[256,256]{1,0:T(8,128)(2,1)}, u32[]{:S(2)}) copy-start(bf16[256,256]{1,0:T(8,128)(2,1)} %param.16) | copy-start | bytes 393220
  29.3 1.0 %copy-start.8 = (bf16[256,256]{1,0:T(8,128)(2,1)S(1)}, bf16[256,256]{1,0:T(8,128)(2,1)}, u32[]{:S(2)}) copy-start(bf16[256,256]{1,0:T(8,128)(2,1)} %param.19) | copy-start | bytes 393220
  29.7 6.2 %copy-start.3 = (bf16[3,3,256,256]{3,2,1,0:T(8,128)(2,1)S(1)}, bf16[3,3,256,256]{3,2,1,0:T(8,128)(2,1)}, u32[]{:S(2)}) copy-start(bf16[3,3,256,256]{3,2,1,0:T(8,128)(2,1)} %param.21) | copy-start | bytes 3538948
  30.6 5.5 %collective-permute-start.5 = (bf16[8,4,1,256]{3,2,1,0:T(2,128)(2,1)S(1)}, bf16[8,4,1,256]{3,2,1,0:T(2,128)(2,1)S(1)}, u32[]{:S(2)}, u32[]{:S(2)}) collective-permute-start(bf16[8,4,1,256]{3,2,1,0:T(2,128)(2,1)S(1)} %get-tuple-element.30), channel_id=1, source_target_pairs={{8,0},{16,8},{24,16},{9,1},{17,9},{25,17},{10,2},{18,10},{26,18},{... | collective-permute-start | bytes 49160 | tf_op jit(solution)/shard_map/ppermute | solution.py:18
  33.4 5.6 %collective-permute-start.4 = (bf16[8,4,1,256]{3,2,1,0:T(2,128)(2,1)S(1)}, bf16[8,4,1,256]{3,2,1,0:T(2,128)(2,1)S(1)}, u32[]{:S(2)}, u32[]{:S(2)}) collective-permute-start(bf16[8,4,1,256]{3,2,1,0:T(2,128)(2,1)S(1)} %get-tuple-element.29), channel_id=1, source_target_pairs={{0,8},{8,16},{16,24},{1,9},{9,17},{17,25},{2,10},{10,18},{18,26},{... | collective-permute-start | bytes 49160 | tf_op jit(solution)/shard_map/ppermute | solution.py:16
  39.0 9.2 %collective-permute-start.6 = (bf16[8,1,10,256]{3,2,1,0:T(8,128)(2,1)S(1)}, bf16[8,1,10,256]{3,2,1,0:T(8,128)(2,1)S(1)}, u32[]{:S(2)}, u32[]{:S(2)}) collective-permute-start(bf16[8,1,10,256]{3,2,1,0:T(8,128)(2,1)S(1)} %get-tuple-element.25), channel_id=1, source_target_pairs={{0,1},{1,2},{2,3},{3,4},{4,5},{5,6},{6,7},{8,9},{9,10},{10,11},{11... | collective-permute-start | bytes 122888 | tf_op jit(solution)/shard_map/ppermute | solution.py:16
  46.1 5.6 %collective-permute-start.7 = (bf16[8,1,10,256]{3,2,1,0:T(8,128)(2,1)S(1)}, bf16[8,1,10,256]{3,2,1,0:T(8,128)(2,1)S(1)}, u32[]{:S(2)}, u32[]{:S(2)}) collective-permute-start(bf16[8,1,10,256]{3,2,1,0:T(8,128)(2,1)S(1)} %get-tuple-element.26), channel_id=1, source_target_pairs={{1,0},{2,1},{3,2},{4,3},{5,4},{6,5},{7,6},{9,8},{10,9},{11,10},{12... | collective-permute-start | bytes 122888 | tf_op jit(solution)/shard_map/ppermute | solution.py:18
where the time goes:
time: 54.8 us; the launch traced here: 54.3 us
  starting transfers between devices  29.9 us (55%)
  waiting for transfers between devices  11.6 us (21%)
  matrix products  7.61 us (14%)
  local copies, waits for them, and re-layouts  2.71 us (5%)
  other arithmetic  1.94 us (4%)
  between operations  0.57 us (1%)
    ppermute x4, starting transfers between devices, extended(): lax.ppermute(tail, axis, [(i, (i + 1) % count) for i in range(ends)])  15.8 us
    ppermute x4, starting transfers between devices, extended(): lax.ppermute(head, axis, [((i + 1) % count, i) for i in range(ends)])  10.5 us
    dot_general x27, matrix products, spatial(): jnp.dot(window.reshape(-1, channels), weight[row_tap, col_tap], preferred...  5.71 us
    ppermute x4, waiting for transfers between devices, extended(): lax.ppermute(tail, axis, [(i, (i + 1) % count) for i in range(ends)])  4.84 us
    all_to_all x1, starting transfers between devices, on_device(): lax.all_to_all(second, 'frame', split_axis=2, concat_axis=0, tiled=True)  3.67 us
    ppermute x4, waiting for transfers between devices, extended(): lax.ppermute(head, axis, [((i + 1) % count, i) for i in range(ends)])  3.52 us
    all_to_all x1, waiting for transfers between devices, on_device(): lax.all_to_all(second, 'frame', split_axis=2, concat_axis=0, tiled=True)  3.27 us
    concatenate x6, other arithmetic, extended(): jnp.concatenate([lax.ppermute(tail, axis, [(i, (i + 1) % count) for i in...  1.53 us
  transfers between devices with their start and end apart: 9, of which 5 were waited for; matrix products, arithmetic and copies ran while one was open for 1% of the time, Pallas kernels for 0%

commit v1 on v0

--- a/solution.py
+++ b/solution.py
@@ -3,6 +3,22 @@
 import jax.numpy as jnp
 from jax import lax
 from jax.sharding import PartitionSpec as P
+
+
+def swapped_with_each(x, axis, split, join):
+    ways, here = (lax.axis_size(axis), lax.axis_index(axis))
+    width = x.shape[split] // ways
+    dims = list(x.shape)
+    dims[split] = width
+    height = dims[join]
+    dims[join] = height * ways
+    full = jnp.zeros(dims, x.dtype)
+    for mask in range(ways):
+        part = lax.dynamic_slice_in_dim(x, (here ^ mask) * width, width, axis=split)
+        if mask:
+            part = lax.ppermute(part, axis, [(d, d ^ mask) for d in range(ways)])
+        full = lax.dynamic_update_slice_in_dim(full, part, (here ^ mask) * height, axis=join)
+    return full
 
 
 def extended(cells, sides, width):
@@ -109,7 +125,7 @@
     second = jax.nn.silu(
         spatial(pad_columns(haloed_two), conv_second, row_count, col_whole)
     ).astype(jnp.bfloat16)
-    moved = lax.all_to_all(second, "frame", split_axis=2, concat_axis=0, tiled=True)
+    moved = swapped_with_each(second, "frame", 2, 0)
     attended = temporal(moved, time_kernel, norm_gain, w_query, w_key, w_value, w_out, frame_bias)
     col_count = attended.shape[2]
     framed_last = extended(attended, (("frame", 2), ("row", 1)), 1)

time: 54.8 us -> 52.8 us (0.964)
  starting transfers between devices: 29.9 us -> 28.7 us
  local copies, waits for them, and re-layouts: 2.71 us -> 1.96 us
    all_to_all x1 -> x0, starting transfers between devices: 3.67 us -> none  [on_device(): lax.all_to_all(second, 'frame', split_axis=2, concat_axis=0, tiled=True)]
    all_to_all x1 -> x0, waiting for transfers between devices: 3.27 us -> none  [on_device(): lax.all_to_all(second, 'frame', split_axis=2, concat_axis=0, tiled=True)]
    ppermute x0 -> x3, starting transfers between devices: none -> 2.71 us  [swapped_with_each(): part = lax.ppermute(part, axis, [(d, d ^ mask) for d in range(ways)])]
    ppermute x0 -> x3, waiting for transfers between devices: none -> 2.43 us  [swapped_with_each(): part = lax.ppermute(part, axis, [(d, d ^ mask) for d in range(ways)])]
    ppermute x4, starting transfers between devices: 15.8 us -> 14.9 us  [extended(): lax.ppermute(tail, axis, [(i, (i + 1) % count) for i in range(ends)])]
    ppermute x4, waiting for transfers between devices: 4.84 us -> 5.67 us  [extended(): lax.ppermute(tail, axis, [(i, (i + 1) % count) for i in range(ends)])]
    convert_element_type x1 -> x0, local copies, waits for them, and re-layouts: 0.76 us -> none  [on_device(): second = jax.nn.silu(spatial(pad_columns(haloed_two), conv_second, row_co...]
    ppermute x4, starting transfers between devices: 10.5 us -> 11.1 us  [extended(): lax.ppermute(head, axis, [((i + 1) % count, i) for i in range(ends)])]
  transfers between devices with their start and end apart: 9 -> 11, of which waited for: 5 -> 6; matrix products, arithmetic and copies ran while one was open for 1% -> 1% of each run, Pallas kernels for 0% -> 0%
where the time goes in v1:
time: 52.8 us; the launch traced here: 52.5 us
  starting transfers between devices  28.7 us (54%)
  waiting for transfers between devices  11.6 us (22%)
  matrix products  7.6 us (14%)
  local copies, waits for them, and re-layouts  1.96 us (4%)
  other arithmetic  1.94 us (4%)
  between operations  0.62 us (1%)
    ppermute x4, starting transfers between devices, extended(): lax.ppermute(tail, axis, [(i, (i + 1) % count) for i in range(ends)])  14.9 us
    ppermute x4, starting transfers between devices, extended(): lax.ppermute(head, axis, [((i + 1) % count, i) for i in range(ends)])  11.1 us
    dot_general x27, matrix products, spatial(): jnp.dot(window.reshape(-1, channels), weight[row_tap, col_tap], preferred...  5.72 us
    ppermute x4, waiting for transfers between devices, extended(): lax.ppermute(tail, axis, [(i, (i + 1) % count) for i in range(ends)])  5.67 us
    ppermute x4, waiting for transfers between devices, extended(): lax.ppermute(head, axis, [((i + 1) % count, i) for i in range(ends)])  3.52 us
    ppermute x3, starting transfers between devices, swapped_with_each(): part = lax.ppermute(part, axis, [(d, d ^ mask) for d in range(ways)])  2.71 us
    ppermute x3, waiting for transfers between devices, swapped_with_each(): part = lax.ppermute(part, axis, [(d, d ^ mask) for d in range(ways)])  2.43 us
    concatenate x6, other arithmetic, extended(): jnp.concatenate([lax.ppermute(tail, axis, [(i, (i + 1) % count) for i in...  1.53 us
  transfers between devices with their start and end apart: 11, of which 6 were waited for; matrix products, arithmetic and copies ran while one was open for 1% of the time, Pallas kernels for 0%

profile of v1, /device:TPU:21, one launch (start us, length us, event | category | flops | bytes accessed | tf_op | source)
XLA Modules:
  0.0 52.5 jit_solution(11993837005561786987)
XLA Ops:
  0.0 0.9 %fusion.110 = (bf16[2,1,32,256]{3,2,1,0:T(8,128)(2,1)S(1)}, bf16[2,1,32,256]{3,2,1,0:T(8,128)(2,1)S(1)}) fusion(bf16[2,4,32,256]{3,2,1,0:T(8,128)(2,1)} %param.11), kind=kLoop, calls=%fused_computation.163 | loop fusion | bytes 131072 | tf_op jit(solution)/shard_map/slice | solution.py:29
  0.9 2.6 %collective-permute-start.1 = (bf16[2,1,32,256]{3,2,1,0:T(8,128)(2,1)S(1)}, bf16[2,1,32,256]{3,2,1,0:T(8,128)(2,1)S(1)}, u32[]{:S(2)}, u32[]{:S(2)}) collective-permute-start(bf16[2,1,32,256]{3,2,1,0:T(8,128)(2,1)S(1)} %get-tuple-element.42), channel_id=1, source_target_pairs={{1,0},{2,1},{3,2},{4,3},{5,4},{6,5},{7,6},{9,8},{10,9},{11,10},{12... | collective-permute-start | bytes 98312 | tf_op jit(solution)/shard_map/ppermute | solution.py:34
  3.5 3.1 %collective-permute-start = (bf16[2,1,32,256]{3,2,1,0:T(8,128)(2,1)S(1)}, bf16[2,1,32,256]{3,2,1,0:T(8,128)(2,1)S(1)}, u32[]{:S(2)}, u32[]{:S(2)}) collective-permute-start(bf16[2,1,32,256]{3,2,1,0:T(8,128)(2,1)S(1)} %get-tuple-element.41), channel_id=1, source_target_pairs={{0,1},{1,2},{2,3},{3,4},{4,5},{5,6},{6,7},{8,9},{9,10},{10,11},{11... | collective-permute-start | bytes 98312 | tf_op jit(solution)/shard_map/ppermute | solution.py:32
  6.6 1.0 %collective-permute-done = bf16[2,1,32,256]{3,2,1,0:T(8,128)(2,1)S(1)} collective-permute-done((bf16[2,1,32,256]{3,2,1,0:T(8,128)(2,1)S(1)}, bf16[2,1,32,256]{3,2,1,0:T(8,128)(2,1)S(1)}, u32[]{:S(2)}, u32[]{:S(2)}) %collective-permute-start) | collective-permute-done | bytes 32800 | tf_op jit(solution)/shard_map/ppermute | solution.py:32
  7.6 1.0 %fusion.18 = bf16[2,6,34,256]{3,2,1,0:T(8,128)(2,1)S(1)} fusion(bf16[2,1,32,256]{3,2,1,0:T(8,128)(2,1)S(1)} %collective-permute-done.1, bf16[2,4,32,256]{3,2,1,0:T(8,128)(2,1)} %param.11, bf16[2,1,32,256]{3,2,1,0:T(8,128)(2,1)S(1)} %collective-permute-done), kind=kLoop, calls=%fused_computation.56 | loop fusion | flops 1253376 | bytes 405504 | tf_op jit(solution)/shard_map/concatenate | solution.py:30
  8.6 0.1 fusion.107
  8.7 0.2 fusion.56
  8.9 0.2 fusion.65
  9.1 0.4 copy-done.1
  9.5 0.2 convolution_add_fusion.20
  9.7 0.2 convolution_add_fusion.19
  9.9 0.2 convolution_add_fusion.18
  10.1 0.2 convolution_add_fusion.17
  10.3 0.2 convolution_add_fusion.16
  10.5 0.2 convolution_add_fusion.15
  10.7 0.2 fusion.4
  10.9 0.1 multiply_convert_fusion.2
  11.0 3.2 %collective-permute-start.3 = (bf16[2,1,32,256]{3,2,1,0:T(8,128)(2,1)S(1)}, bf16[2,1,32,256]{3,2,1,0:T(8,128)(2,1)S(1)}, u32[]{:S(2)}, u32[]{:S(2)}) collective-permute-start(bf16[2,1,32,256]{3,2,1,0:T(8,128)(2,1)S(1)} %get-tuple-element.38), channel_id=1, source_target_pairs={{1,0},{2,1},{3,2},{4,3},{5,4},{6,5},{7,6},{9,8},{10,9},{11,10},{12... | collective-permute-start | bytes 98312 | tf_op jit(solution)/shard_map/ppermute | solution.py:34
  14.2 3.1 %collective-permute-start.2 = (bf16[2,1,32,256]{3,2,1,0:T(8,128)(2,1)S(1)}, bf16[2,1,32,256]{3,2,1,0:T(8,128)(2,1)S(1)}, u32[]{:S(2)}, u32[]{:S(2)}) collective-permute-start(bf16[2,1,32,256]{3,2,1,0:T(8,128)(2,1)S(1)} %get-tuple-element.37), channel_id=1, source_target_pairs={{0,1},{1,2},{2,3},{3,4},{4,5},{5,6},{6,7},{8,9},{9,10},{10,11},{11... | collective-permute-start | bytes 98312 | tf_op jit(solution)/shard_map/ppermute | solution.py:32
  17.3 1.0 %collective-permute-done.2 = bf16[2,1,32,256]{3,2,1,0:T(8,128)(2,1)S(1)} collective-permute-done((bf16[2,1,32,256]{3,2,1,0:T(8,128)(2,1)S(1)}, bf16[2,1,32,256]{3,2,1,0:T(8,128)(2,1)S(1)}, u32[]{:S(2)}, u32[]{:S(2)}) %collective-permute-start.2) | collective-permute-done | bytes 32800 | tf_op jit(solution)/shard_map/ppermute | solution.py:32
  18.4 0.1 fusion.106
  18.5 0.2 fusion.45
  18.7 0.2 fusion.54
  18.9 0.2 convolution_add_fusion.13
  19.1 0.2 convolution_add_fusion.12
  19.3 0.2 convolution_add_fusion.11
  19.5 0.2 convolution_add_fusion.10
  19.7 0.2 convolution_add_fusion.9
  19.9 0.2 convolution_add_fusion.8
  20.1 0.2 fusion.3
  20.5 1.3 %collective-permute-start.4 = (bf16[2,4,8,256]{3,2,1,0:T(8,128)(2,1)S(1)}, bf16[2,4,8,256]{3,2,1,0:T(8,128)(2,1)S(1)}, u32[]{:S(2)}, u32[]{:S(2)}) collective-permute-start(bf16[2,4,8,256]{3,2,1,0:T(8,128)(2,1)S(1)} %get-tuple-element.33), channel_id=1, source_target_pairs={{0,8},{8,0},{16,24},{24,16},{1,9},{9,1},{17,25},{25,17},{2,10},{10... | collective-permute-start | bytes 98312 | tf_op jit(solution)/shard_map/ppermute | solution.py:19
  21.8 0.2 collective-permute-start.5
  22.0 1.2 %collective-permute-start.6 = (bf16[2,4,8,256]{3,2,1,0:T(8,128)(2,1)S(1)}, bf16[2,4,8,256]{3,2,1,0:T(8,128)(2,1)S(1)}, u32[]{:S(2)}, u32[]{:S(2)}) collective-permute-start(bf16[2,4,8,256]{3,2,1,0:T(8,128)(2,1)S(1)} %get-tuple-element.31), channel_id=1, source_target_pairs={{0,24},{8,16},{16,8},{24,0},{1,25},{9,17},{17,9},{25,1},{2,26},{10... | collective-permute-start | bytes 98312 | tf_op jit(solution)/shard_map/ppermute | solution.py:19
  23.3 1.6 %collective-permute-done.5 = bf16[2,4,8,256]{3,2,1,0:T(8,128)(2,1)S(1)} collective-permute-done((bf16[2,4,8,256]{3,2,1,0:T(8,128)(2,1)S(1)}, bf16[2,4,8,256]{3,2,1,0:T(8,128)(2,1)S(1)}, u32[]{:S(2)}, u32[]{:S(2)}) %collective-permute-start.5) | collective-permute-done | bytes 32800 | tf_op jit(solution)/shard_map/ppermute | solution.py:19
  24.9 0.8 %collective-permute-done.6 = bf16[2,4,8,256]{3,2,1,0:T(8,128)(2,1)S(1)} collective-permute-done((bf16[2,4,8,256]{3,2,1,0:T(8,128)(2,1)S(1)}, bf16[2,4,8,256]{3,2,1,0:T(8,128)(2,1)S(1)}, u32[]{:S(2)}, u32[]{:S(2)}) %collective-permute-start.6) | collective-permute-done | bytes 32800 | tf_op jit(solution)/shard_map/ppermute | solution.py:19
  25.7 0.2 fusion.38
  25.9 0.2 fusion.40
  26.1 0.3 fusion.11
  26.4 0.1 fusion.13
  26.5 0.2 convolution_convert_fusion.2
  26.8 0.2 convolution_convert_fusion
  27.0 0.2 convolution_convert_fusion.1
  27.2 0.3 fusion.9
  27.5 0.1 fusion.111
  27.5 0.3 fusion.67
  27.8 0.2 fusion.5
  28.1 3.4 %collective-permute-start.8 = (bf16[8,4,1,256]{3,2,1,0:T(2,128)(2,1)S(1)}, bf16[8,4,1,256]{3,2,1,0:T(2,128)(2,1)S(1)}, u32[]{:S(2)}, u32[]{:S(2)}) collective-permute-start(bf16[8,4,1,256]{3,2,1,0:T(2,128)(2,1)S(1)} %get-tuple-element.30), channel_id=1, source_target_pairs={{8,0},{16,8},{24,16},{9,1},{17,9},{25,17},{10,2},{18,10},{26,18},{... | collective-permute-start | bytes 49160 | tf_op jit(solution)/shard_map/ppermute | solution.py:34
  31.5 1.9 %collective-permute-start.7 = (bf16[8,4,1,256]{3,2,1,0:T(2,128)(2,1)S(1)}, bf16[8,4,1,256]{3,2,1,0:T(2,128)(2,1)S(1)}, u32[]{:S(2)}, u32[]{:S(2)}) collective-permute-start(bf16[8,4,1,256]{3,2,1,0:T(2,128)(2,1)S(1)} %get-tuple-element.29), channel_id=1, source_target_pairs={{0,8},{8,16},{16,24},{1,9},{9,17},{17,25},{2,10},{10,18},{18,26},{... | collective-permute-start | bytes 49160 | tf_op jit(solution)/shard_map/ppermute | solution.py:32
  33.4 0.2 fusion.26
  33.6 3.7 %collective-permute-done.7 = bf16[8,4,1,256]{3,2,1,0:T(2,128)(2,1)S(1)} collective-permute-done((bf16[8,4,1,256]{3,2,1,0:T(2,128)(2,1)S(1)}, bf16[8,4,1,256]{3,2,1,0:T(2,128)(2,1)S(1)}, u32[]{:S(2)}, u32[]{:S(2)}) %collective-permute-start.7) | collective-permute-done | bytes 16416 | tf_op jit(solution)/shard_map/ppermute | solution.py:32
  37.4 6.8 %collective-permute-start.9 = (bf16[8,1,10,256]{3,2,1,0:T(8,128)(2,1)S(1)}, bf16[8,1,10,256]{3,2,1,0:T(8,128)(2,1)S(1)}, u32[]{:S(2)}, u32[]{:S(2)}) collective-permute-start(bf16[8,1,10,256]{3,2,1,0:T(8,128)(2,1)S(1)} %get-tuple-element.25), channel_id=1, source_target_pairs={{0,1},{1,2},{2,3},{3,4},{4,5},{5,6},{6,7},{8,9},{9,10},{10,11},{11... | collective-permute-start | bytes 122888 | tf_op jit(solution)/shard_map/ppermute | solution.py:32
  44.2 1.9 %collective-permute-start.10 = (bf16[8,1,10,256]{3,2,1,0:T(8,128)(2,1)S(1)}, bf16[8,1,10,256]{3,2,1,0:T(8,128)(2,1)S(1)}, u32[]{:S(2)}, u32[]{:S(2)}) collective-permute-start(bf16[8,1,10,256]{3,2,1,0:T(8,128)(2,1)S(1)} %get-tuple-element.26), channel_id=1, source_target_pairs={{1,0},{2,1},{3,2},{4,3},{5,4},{6,5},{7,6},{9,8},{10,9},{11,10},{12... | collective-permute-start | bytes 122888 | tf_op jit(solution)/shard_map/ppermute | solution.py:34
  46.1 0.1 pad_maximum_fusion.1
  46.3 3.5 %collective-permute-done.10 = bf16[8,1,10,256]{3,2,1,0:T(8,128)(2,1)S(1)} collective-permute-done((bf16[8,1,10,256]{3,2,1,0:T(8,128)(2,1)S(1)}, bf16[8,1,10,256]{3,2,1,0:T(8,128)(2,1)S(1)}, u32[]{:S(2)}, u32[]{:S(2)}) %collective-permute-start.10) | collective-permute-done | bytes 40992 | tf_op jit(solution)/shard_map/ppermute | solution.py:34
  49.8 0.3 maximum_maximum_fusion
  50.1 0.2 fusion.104
  50.2 0.2 fusion.23
  50.4 0.2 fusion.30
  50.6 0.2 convolution_add_fusion.5
  50.8 0.2 convolution_add_fusion.4
  51.0 0.2 fusion.2
  51.2 0.2 fusion.1
  51.4 0.2 convolution_add_fusion.1
  51.6 0.8 %fusion.6 = bf16[256,256]{1,0:T(8,128)(2,1)} fusion(f32[256,256]{1,0:T(8,128)S(1)} %convolution_add_fusion.1, bf16[256,256]{1,0:T(8,128)(2,1)S(1)} %bitcast.191, bf16[3,3,256,256]{3,2,1,0:T(8,128)(2,1)S(1)} %copy-done.3), kind=kOutput, calls=%fused_computation.27 | convolution fusion | flops 33685504 | bytes 655360 | tf_op jit(solution)/shard_map/dot_general | solution.py:47
  (40 shorter events, 0.6 us)
Async XLA Ops:
  0.0 26.5 %copy-start = (bf16[256,256]{1,0:T(8,128)(2,1)S(1)}, bf16[256,256]{1,0:T(8,128)(2,1)}, u32[]{:S(2)}) copy-start(bf16[256,256]{1,0:T(8,128)(2,1)} %param.18) | copy-start | bytes 393220
  0.0 8.7 %copy-start.2 = (bf16[3,3,256,256]{3,2,1,0:T(8,128)(2,1)S(1)}, bf16[3,3,256,256]{3,2,1,0:T(8,128)(2,1)}, u32[]{:S(2)}) copy-start(bf16[3,3,256,256]{3,2,1,0:T(8,128)(2,1)} %param.12) | copy-start | bytes 3538948
  0.9 5.7 %collective-permute-start.1 = (bf16[2,1,32,256]{3,2,1,0:T(8,128)(2,1)S(1)}, bf16[2,1,32,256]{3,2,1,0:T(8,128)(2,1)S(1)}, u32[]{:S(2)}, u32[]{:S(2)}) collective-permute-start(bf16[2,1,32,256]{3,2,1,0:T(8,128)(2,1)S(1)} %get-tuple-element.42), channel_id=1, source_target_pairs={{1,0},{2,1},{3,2},{4,3},{5,4},{6,5},{7,6},{9,8},{10,9},{11,10},{12... | collective-permute-start | bytes 98312 | tf_op jit(solution)/shard_map/ppermute | solution.py:34
  3.5 4.1 %collective-permute-start = (bf16[2,1,32,256]{3,2,1,0:T(8,128)(2,1)S(1)}, bf16[2,1,32,256]{3,2,1,0:T(8,128)(2,1)S(1)}, u32[]{:S(2)}, u32[]{:S(2)}) collective-permute-start(bf16[2,1,32,256]{3,2,1,0:T(8,128)(2,1)S(1)} %get-tuple-element.41), channel_id=1, source_target_pairs={{0,1},{1,2},{2,3},{3,4},{4,5},{5,6},{6,7},{8,9},{9,10},{10,11},{11... | collective-permute-start | bytes 98312 | tf_op jit(solution)/shard_map/ppermute | solution.py:32
  8.6 0.9 %copy-start.1 = (bf16[2,4,32,256]{3,2,1,0:T(8,128)(2,1)S(1)}, bf16[2,4,32,256]{3,2,1,0:T(8,128)(2,1)}, u32[]{:S(2)}) copy-start(bf16[2,4,32,256]{3,2,1,0:T(8,128)(2,1)} %param.11) | copy-start | bytes 393220
  10.9 7.5 %copy-start.4 = (bf16[3,3,256,256]{3,2,1,0:T(8,128)(2,1)S(1)}, bf16[3,3,256,256]{3,2,1,0:T(8,128)(2,1)}, u32[]{:S(2)}) copy-start(bf16[3,3,256,256]{3,2,1,0:T(8,128)(2,1)} %param.13) | copy-start | bytes 3538948
  11.0 6.3 %collective-permute-start.3 = (bf16[2,1,32,256]{3,2,1,0:T(8,128)(2,1)S(1)}, bf16[2,1,32,256]{3,2,1,0:T(8,128)(2,1)S(1)}, u32[]{:S(2)}, u32[]{:S(2)}) collective-permute-start(bf16[2,1,32,256]{3,2,1,0:T(8,128)(2,1)S(1)} %get-tuple-element.38), channel_id=1, source_target_pairs={{1,0},{2,1},{3,2},{4,3},{5,4},{6,5},{7,6},{9,8},{10,9},{11,10},{12... | collective-permute-start | bytes 98312 | tf_op jit(solution)/shard_map/ppermute | solution.py:34
  14.2 4.1 %collective-permute-start.2 = (bf16[2,1,32,256]{3,2,1,0:T(8,128)(2,1)S(1)}, bf16[2,1,32,256]{3,2,1,0:T(8,128)(2,1)S(1)}, u32[]{:S(2)}, u32[]{:S(2)}) collective-permute-start(bf16[2,1,32,256]{3,2,1,0:T(8,128)(2,1)S(1)} %get-tuple-element.37), channel_id=1, source_target_pairs={{0,1},{1,2},{2,3},{3,4},{4,5},{5,6},{6,7},{8,9},{9,10},{10,11},{11... | collective-permute-start | bytes 98312 | tf_op jit(solution)/shard_map/ppermute | solution.py:32
  19.9 1.8 %copy-start.9 = (f32[8,8]{1,0:T(8,128)S(1)}, f32[8,8]{1,0:T(8,128)}, u32[]{:S(2)}) copy-start(f32[8,8]{1,0:T(8,128)} %param.20) | copy-start | bytes 772
  20.1 5.6 %copy-start.5 = (bf16[3,256,256]{2,1,0:T(8,128)(2,1)S(1)}, bf16[3,256,256]{2,1,0:T(8,128)(2,1)}, u32[]{:S(2)}) copy-start(bf16[3,256,256]{2,1,0:T(8,128)(2,1)} %param.14) | copy-start | bytes 1179652
  20.4 6.0 %copy-start.10 = (f32[256]{0:T(256)S(1)}, f32[256]{0:T(256)}, u32[]{:S(2)}) copy-start(f32[256]{0:T(256)} %param.15) | copy-start | bytes 3076
  20.5 2.8 %collective-permute-start.4 = (bf16[2,4,8,256]{3,2,1,0:T(8,128)(2,1)S(1)}, bf16[2,4,8,256]{3,2,1,0:T(8,128)(2,1)S(1)}, u32[]{:S(2)}, u32[]{:S(2)}) collective-permute-start(bf16[2,4,8,256]{3,2,1,0:T(8,128)(2,1)S(1)} %get-tuple-element.33), channel_id=1, source_target_pairs={{0,8},{8,0},{16,24},{24,16},{1,9},{9,1},{17,25},{25,17},{2,10},{10... | collective-permute-start | bytes 98312 | tf_op jit(solution)/shard_map/ppermute | solution.py:19
  21.8 3.1 %collective-permute-start.5 = (bf16[2,4,8,256]{3,2,1,0:T(8,128)(2,1)S(1)}, bf16[2,4,8,256]{3,2,1,0:T(8,128)(2,1)S(1)}, u32[]{:S(2)}, u32[]{:S(2)}) collective-permute-start(bf16[2,4,8,256]{3,2,1,0:T(8,128)(2,1)S(1)} %get-tuple-element.32), channel_id=1, source_target_pairs={{0,16},{8,24},{16,0},{24,8},{1,17},{9,25},{17,1},{25,9},{2,18},{10... | collective-permute-start | bytes 98312 | tf_op jit(solution)/shard_map/ppermute | solution.py:19
  22.0 3.7 %collective-permute-start.6 = (bf16[2,4,8,256]{3,2,1,0:T(8,128)(2,1)S(1)}, bf16[2,4,8,256]{3,2,1,0:T(8,128)(2,1)S(1)}, u32[]{:S(2)}, u32[]{:S(2)}) collective-permute-start(bf16[2,4,8,256]{3,2,1,0:T(8,128)(2,1)S(1)} %get-tuple-element.31), channel_id=1, source_target_pairs={{0,24},{8,16},{16,8},{24,0},{1,25},{9,17},{17,9},{25,1},{2,26},{10... | collective-permute-start | bytes 98312 | tf_op jit(solution)/shard_map/ppermute | solution.py:19
  25.9 0.9 %copy-start.6 = (bf16[256,256]{1,0:T(8,128)(2,1)S(1)}, bf16[256,256]{1,0:T(8,128)(2,1)}, u32[]{:S(2)}) copy-start(bf16[256,256]{1,0:T(8,128)(2,1)} %param.17) | copy-start | bytes 393220
  25.9 1.1 %copy-start.7 = (bf16[256,256]{1,0:T(8,128)(2,1)S(1)}, bf16[256,256]{1,0:T(8,128)(2,1)}, u32[]{:S(2)}) copy-start(bf16[256,256]{1,0:T(8,128)(2,1)} %param.16) | copy-start | bytes 393220
  26.8 1.0 %copy-start.8 = (bf16[256,256]{1,0:T(8,128)(2,1)S(1)}, bf16[256,256]{1,0:T(8,128)(2,1)}, u32[]{:S(2)}) copy-start(bf16[256,256]{1,0:T(8,128)(2,1)} %param.19) | copy-start | bytes 393220
  27.2 6.2 %copy-start.3 = (bf16[3,3,256,256]{3,2,1,0:T(8,128)(2,1)S(1)}, bf16[3,3,256,256]{3,2,1,0:T(8,128)(2,1)}, u32[]{:S(2)}) copy-start(bf16[3,3,256,256]{3,2,1,0:T(8,128)(2,1)} %param.21) | copy-start | bytes 3538948
  28.1 5.6 %collective-permute-start.8 = (bf16[8,4,1,256]{3,2,1,0:T(2,128)(2,1)S(1)}, bf16[8,4,1,256]{3,2,1,0:T(2,128)(2,1)S(1)}, u32[]{:S(2)}, u32[]{:S(2)}) collective-permute-start(bf16[8,4,1,256]{3,2,1,0:T(2,128)(2,1)S(1)} %get-tuple-element.30), channel_id=1, source_target_pairs={{8,0},{16,8},{24,16},{9,1},{17,9},{25,17},{10,2},{18,10},{26,18},{... | collective-permute-start | bytes 49160 | tf_op jit(solution)/shard_map/ppermute | solution.py:34
  31.5 5.8 %collective-permute-start.7 = (bf16[8,4,1,256]{3,2,1,0:T(2,128)(2,1)S(1)}, bf16[8,4,1,256]{3,2,1,0:T(2,128)(2,1)S(1)}, u32[]{:S(2)}, u32[]{:S(2)}) collective-permute-start(bf16[8,4,1,256]{3,2,1,0:T(2,128)(2,1)S(1)} %get-tuple-element.29), channel_id=1, source_target_pairs={{0,8},{8,16},{16,24},{1,9},{9,17},{17,25},{2,10},{10,18},{18,26},{... | collective-permute-start | bytes 49160 | tf_op jit(solution)/shard_map/ppermute | solution.py:32
  37.4 8.9 %collective-permute-start.9 = (bf16[8,1,10,256]{3,2,1,0:T(8,128)(2,1)S(1)}, bf16[8,1,10,256]{3,2,1,0:T(8,128)(2,1)S(1)}, u32[]{:S(2)}, u32[]{:S(2)}) collective-permute-start(bf16[8,1,10,256]{3,2,1,0:T(8,128)(2,1)S(1)} %get-tuple-element.25), channel_id=1, source_target_pairs={{0,1},{1,2},{2,3},{3,4},{4,5},{5,6},{6,7},{8,9},{9,10},{10,11},{11... | collective-permute-start | bytes 122888 | tf_op jit(solution)/shard_map/ppermute | solution.py:32
  44.2 5.6 %collective-permute-start.10 = (bf16[8,1,10,256]{3,2,1,0:T(8,128)(2,1)S(1)}, bf16[8,1,10,256]{3,2,1,0:T(8,128)(2,1)S(1)}, u32[]{:S(2)}, u32[]{:S(2)}) collective-permute-start(bf16[8,1,10,256]{3,2,1,0:T(8,128)(2,1)S(1)} %get-tuple-element.26), channel_id=1, source_target_pairs={{1,0},{2,1},{3,2},{4,3},{5,4},{6,5},{7,6},{9,8},{10,9},{11,10},{12... | collective-permute-start | bytes 122888 | tf_op jit(solution)/shard_map/ppermute | solution.py:34
